TPU v7x, 32 devices: a whole 2x2x4 slice. The times are simulated.
32 devices in a mesh: vec: 8 (over z, core), rep: 4 (over y, x).
Axes of the slice: x: 2, y: 2, z: 4, core: 2. Of those that a mesh axis runs over, the one named last changes fastest.
Arguments:
- vectors: bfloat16 [1024, 1024], P('vec'), may hold values from 0 to 2
- pivot_index: int32 [4, 8], P('rep'), may hold values from 0 to 1023
Outputs:
- similarity: bfloat16 [7, 32, 1024, 128], P(None, 'rep', 'vec')
All inputs are finite; a program needn't handle non-finite values.
Results may differ from a plain program's by a relative error of at most 0.011.
Values may be sent and summed in bfloat16 or wider, within the bound.
A program may use at most 64 MiB of HBM per device.

v0:
```python
import math

import jax
import jax.numpy as jnp
from jax import lax
from jax.sharding import PartitionSpec as P

HALF = 3


def from_behind(block, axis, distance):
    devices = range(lax.axis_size(axis))
    route = [((i - distance) % len(devices), i) for i in devices]
    return lax.ppermute(block, axis, route)


def contract(left, right):
    return lax.dot_general(
        left, right, (((1,), (1,)), ((), ())), preferred_element_type=jnp.float32
    )


def on_device(vectors, pivot_index):
    block_rows, fields = vectors.shape
    position = lax.axis_index("vec")
    wanted = pivot_index.reshape(-1) - position * block_rows
    columns = jnp.arange(block_rows, dtype=jnp.int32)
    onehot = (wanted[:, None] == columns[None, :]).astype(jnp.bfloat16)
    local_rows = jnp.dot(onehot, vectors, preferred_element_type=jnp.float32)
    pivots = lax.psum(local_rows, "vec")
    count = pivots.shape[0]
    centre = jnp.sum(pivots, axis=1) / fields
    scaled = (vectors.astype(jnp.float32)[None, :, :] * pivots[:, None, :]).astype(jnp.bfloat16)
    scaled = scaled.reshape(count * block_rows, fields)
    replicas = lax.axis_size("rep")
    share = block_rows // replicas
    own_rows = lax.dynamic_slice_in_dim(vectors, lax.axis_index("rep") * share, share, 0)
    window = 2 * HALF + 1
    triples = [None] * window
    grams = [None] * window
    triples[HALF] = contract(scaled, vectors)
    grams[HALF] = contract(own_rows, vectors)
    lower = vectors
    upper = vectors
    for reach in range(1, HALF + 1):
        lower = from_behind(lower, "vec", 1)
        upper = from_behind(upper, "vec", -1)
        triples[HALF - reach] = contract(scaled, lower)
        grams[HALF - reach] = contract(own_rows, lower)
        triples[HALF + reach] = contract(scaled, upper)
        grams[HALF + reach] = contract(own_rows, upper)
    triple_all = jnp.stack(triples).reshape(window, count, block_rows, block_rows)
    gram_all = jnp.stack(grams)
    gram_all = lax.all_gather(gram_all, "rep", axis=1, tiled=True)
    similarity = (triple_all - centre[None, :, None, None] * gram_all[:, None, :, :]) / math.sqrt(
        fields
    )
    return similarity.astype(jnp.bfloat16)


def solution(mesh):
    in_specs = (P("vec", None), P("rep", None))
    out_specs = P(None, "rep", "vec", None)
    return jax.shard_map(
        on_device, mesh=mesh, in_specs=in_specs, out_specs=out_specs, check_vma=False
    )
```

profile of v0, /device:TPU:0, one launch (start us, length us, event | category | flops | bytes accessed | tf_op | source)
XLA Modules:
  0.0 71.4 jit_solution(5123657337619987184)
XLA Ops:
  0.0 0.5 collective-permute-start
  0.5 4.0 %collective-permute-start.3 = (bf16[128,1024]{1,0:T(8,128)(2,1)}, bf16[128,1024]{1,0:T(8,128)(2,1)S(1)}, u32[]{:S(2)}, u32[]{:S(2)}) collective-permute-start(bf16[128,1024]{1,0:T(8,128)(2,1)} %param.2), channel_id=1, source_target_pairs={{4,0},{8,4},{12,8},{16,12},{20,16},{24,20},{28,24},{0,28},{5,1},{9... | collective-permute-start | bytes 786440 | tf_op jit(solution)/shard_map/ppermute | solution.py:14
  4.5 4.5 %collective-permute-done = bf16[128,1024]{1,0:T(8,128)(2,1)S(1)} collective-permute-done((bf16[128,1024]{1,0:T(8,128)(2,1)}, bf16[128,1024]{1,0:T(8,128)(2,1)S(1)}, u32[]{:S(2)}, u32[]{:S(2)}) %collective-permute-start) | collective-permute-done | bytes 262176 | tf_op jit(solution)/shard_map/ppermute | solution.py:14
  9.0 0.0 collective-permute-start.1
  9.0 0.7 subtract_bitcast_fusion
  9.7 0.0 collective-permute-done.3
  9.7 3.5 %collective-permute-start.4 = (bf16[128,1024]{1,0:T(8,128)(2,1)S(1)}, bf16[128,1024]{1,0:T(8,128)(2,1)S(1)}, u32[]{:S(2)}, u32[]{:S(2)}) collective-permute-start(bf16[128,1024]{1,0:T(8,128)(2,1)S(1)} %collective-permute-done.3), channel_id=1, source_target_pairs={{4,0},{8,4},{12,8},{16,12},{20,16},{24,20},{28,24},{0,28},{5,1},{9... | collective-permute-start | bytes 786440 | tf_op jit(solution)/shard_map/ppermute | solution.py:14
  13.2 3.5 %collective-permute-done.1 = bf16[128,1024]{1,0:T(8,128)(2,1)S(1)} collective-permute-done((bf16[128,1024]{1,0:T(8,128)(2,1)S(1)}, bf16[128,1024]{1,0:T(8,128)(2,1)S(1)}, u32[]{:S(2)}, u32[]{:S(2)}) %collective-permute-start.1) | collective-permute-done | bytes 262176 | tf_op jit(solution)/shard_map/ppermute | solution.py:14
  16.7 0.0 collective-permute-start.2
  16.7 1.1 %fusion.56 = f32[8,1024]{1,0:T(8,128)S(1)} fusion(bf16[128,1024]{1,0:T(8,128)(2,1)} %param.2, s32[8]{0:T(128)S(1)} %subtract_bitcast_fusion), kind=kOutput, calls=%fused_computation.66 | convolution fusion | flops 2098176 | bytes 294944 | tf_op jit(solution)/shard_map/dot_general | solution.py:29
  17.8 1.0 %convert_element_type.21 = f32[128,1024]{1,0:T(8,128)S(1)} convert(bf16[128,1024]{1,0:T(8,128)(2,1)} %param.2) | non-fusion elementwise | flops 131072 | bytes 786432 | tf_op jit(solution)/shard_map/convert_element_type | solution.py:33
  18.8 29.4 %psum.7 = f32[8,1024]{1,0:T(8,128)S(1)} all-reduce(f32[8,1024]{1,0:T(8,128)S(1)} %fusion.56), channel_id=1, replica_groups=mesh['vec'=8,'rep'=4] {'vec'}, use_global_device_ids=true, to_apply=%region_0.0 | all-reduce | flops 8192 | bytes 65536 | tf_op jit(solution)/shard_map/psum | solution.py:30
  48.3 0.1 reduce_sum.9
  48.4 0.0 collective-permute-done.4
  48.4 0.1 collective-permute-start.5
  48.5 1.0 %fusion.41 = f32[7,32,128]{2,1,0:T(8,128)S(1)} fusion(bf16[128,1024]{1,0:T(8,128)(2,1)S(1)} %collective-permute-done.2, bf16[128,1024]{1,0:T(8,128)(2,1)} %param.2, s32[]{:T(128)S(6)} %select_n.3), kind=kOutput, calls=%fused_computation.50 | convolution fusion | flops 8388607 | bytes 344068 | tf_op jit(solution)/shard_map/dot_general | solution.py:18
  49.5 1.0 %fusion.40 = f32[7,32,128]{2,1,0:T(8,128)S(1)} fusion(f32[7,32,128]{2,1,0:T(8,128)S(1)} %fusion.41, bf16[128,1024]{1,0:T(8,128)(2,1)S(1)} %collective-permute-done.1, bf16[128,1024]{1,0:T(8,128)(2,1)} %param.2, s32[]{:T(128)S(6)} %select_n.3), kind=kOutput, calls=%fused_computation.48 | convolution fusion | flops 8388608 | bytes 344068 | tf_op jit(solution)/shard_map/dot_general | solution.py:18
  50.5 1.0 %fusion.39 = f32[7,32,128]{2,1,0:T(8,128)S(1)} fusion(f32[7,32,128]{2,1,0:T(8,128)S(1)} %fusion.40, bf16[128,1024]{1,0:T(8,128)(2,1)S(1)} %collective-permute-done, bf16[128,1024]{1,0:T(8,128)(2,1)} %param.2, s32[]{:T(128)S(6)} %select_n.3), kind=kOutput, calls=%fused_computation.46 | convolution fusion | flops 8388608 | bytes 344068 | tf_op jit(solution)/shard_map/dot_general | solution.py:18
  51.6 1.2 %fusion.38 = f32[7,32,128]{2,1,0:T(8,128)S(1)} fusion(f32[7,32,128]{2,1,0:T(8,128)S(1)} %fusion.39, bf16[128,1024]{1,0:T(8,128)(2,1)} %param.2, s32[]{:T(128)S(6)} %select_n.3), kind=kOutput, calls=%fused_computation.44 | convolution fusion | flops 8388608 | bytes 344068 | tf_op jit(solution)/shard_map/dot_general | solution.py:18
  52.8 0.7 %fusion.22 = f32[7,8,128,128]{3,2,1,0:T(8,128)S(1)} fusion(f32[8,1024]{1,0:T(8,128)S(1)} %psum.7, f32[128,1024]{1,0:T(8,128)S(1)} %convert_element_type.21, bf16[128,1024]{1,0:T(8,128)(2,1)S(1)} %collective-permute-done.2), kind=kOutput, calls=%fused_computation.24 | convolution fusion | flops 270532608 | bytes 1343488 | tf_op jit(solution)/shard_map/dot_general | solution.py:18
  53.6 0.7 fusion.24
  54.3 0.7 fusion.26
  55.0 0.2 fusion.37
  55.2 0.2 fusion.36
  55.4 0.7 %fusion.28 = f32[7,8,128,128]{3,2,1,0:T(8,128)S(1)} fusion(f32[7,8,128,128]{3,2,1,0:T(8,128)S(1)} %fusion.26, f32[8,1024]{1,0:T(8,128)S(1)} %psum.7, f32[128,1024]{1,0:T(8,128)S(1)} %convert_element_type.21, bf16[128,1024]{1,0:T(8,128)(2,1)S(1)} %copy-done), kind=kOutput, calls=%fused_computation.30 | convolution fusion | flops 270532608 | bytes 1343488 | tf_op jit(solution)/shard_map/dot_general | solution.py:18
  56.1 0.0 collective-permute-done.5
  56.1 0.2 fusion.35
  56.3 11.0 %all_gather.3 = f32[7,128,128]{2,1,0:T(8,128)S(1)} all-gather(f32[7,32,128]{2,1,0:T(8,128)S(1)} %fusion.35), channel_id=1, replica_groups=mesh['vec'=8,'rep'=4] {'rep'}, dimensions={1}, use_global_device_ids=true | all-gather | bytes 573440 | tf_op jit(solution)/shard_map/all_gather | solution.py:54
  67.3 0.7 fusion.30
  68.0 0.7 fusion.32
  68.8 0.7 fusion.34
  69.5 1.9 %multiply_convert_fusion.8 = bf16[7,8,128,128]{3,2,1,0:T(8,128)(2,1)} fusion(f32[7,8,128,128]{3,2,1,0:T(8,128)S(1)} %fusion.34, f32[7,128,128]{2,1,0:T(8,128)S(1)} %all_gather.3, f32[8]{0:T(128)S(1)} %broadcast_multiply_fusion), kind=kLoop, calls=%fused_computation.8 | loop fusion | flops 3670016 | bytes 5963808 | tf_op jit(solution)/shard_map/convert_element_type | solution.py:58
  (4 shorter events, 0.0 us)
Async XLA Ops:
  0.0 9.0 %collective-permute-start = (bf16[128,1024]{1,0:T(8,128)(2,1)}, bf16[128,1024]{1,0:T(8,128)(2,1)S(1)}, u32[]{:S(2)}, u32[]{:S(2)}) collective-permute-start(bf16[128,1024]{1,0:T(8,128)(2,1)} %param.2), channel_id=1, source_target_pairs={{28,0},{0,4},{4,8},{8,12},{12,16},{16,20},{20,24},{24,28},{29,1},{... | collective-permute-start | bytes 786440 | tf_op jit(solution)/shard_map/ppermute | solution.py:14
  0.5 9.2 %collective-permute-start.3 = (bf16[128,1024]{1,0:T(8,128)(2,1)}, bf16[128,1024]{1,0:T(8,128)(2,1)S(1)}, u32[]{:S(2)}, u32[]{:S(2)}) collective-permute-start(bf16[128,1024]{1,0:T(8,128)(2,1)} %param.2), channel_id=1, source_target_pairs={{4,0},{8,4},{12,8},{16,12},{20,16},{24,20},{28,24},{0,28},{5,1},{9... | collective-permute-start | bytes 786440 | tf_op jit(solution)/shard_map/ppermute | solution.py:14
  9.0 7.7 %collective-permute-start.1 = (bf16[128,1024]{1,0:T(8,128)(2,1)S(1)}, bf16[128,1024]{1,0:T(8,128)(2,1)S(1)}, u32[]{:S(2)}, u32[]{:S(2)}) collective-permute-start(bf16[128,1024]{1,0:T(8,128)(2,1)S(1)} %collective-permute-done), channel_id=1, source_target_pairs={{28,0},{0,4},{4,8},{8,12},{12,16},{16,20},{20,24},{24,28},{29,1},{... | collective-permute-start | bytes 786440 | tf_op jit(solution)/shard_map/ppermute | solution.py:14
  9.7 38.7 %collective-permute-start.4 = (bf16[128,1024]{1,0:T(8,128)(2,1)S(1)}, bf16[128,1024]{1,0:T(8,128)(2,1)S(1)}, u32[]{:S(2)}, u32[]{:S(2)}) collective-permute-start(bf16[128,1024]{1,0:T(8,128)(2,1)S(1)} %collective-permute-done.3), channel_id=1, source_target_pairs={{4,0},{8,4},{12,8},{16,12},{20,16},{24,20},{28,24},{0,28},{5,1},{9... | collective-permute-start | bytes 786440 | tf_op jit(solution)/shard_map/ppermute | solution.py:14
  16.7 31.8 %collective-permute-start.2 = (bf16[128,1024]{1,0:T(8,128)(2,1)S(1)}, bf16[128,1024]{1,0:T(8,128)(2,1)S(1)}, u32[]{:S(2)}, u32[]{:S(2)}) collective-permute-start(bf16[128,1024]{1,0:T(8,128)(2,1)S(1)} %collective-permute-done.1), channel_id=1, source_target_pairs={{28,0},{0,4},{4,8},{8,12},{12,16},{16,20},{20,24},{24,28},{29,1},{... | collective-permute-start | bytes 786440 | tf_op jit(solution)/shard_map/ppermute | solution.py:14
  48.4 7.7 %collective-permute-start.5 = (bf16[128,1024]{1,0:T(8,128)(2,1)S(1)}, bf16[128,1024]{1,0:T(8,128)(2,1)S(1)}, u32[]{:S(2)}, u32[]{:S(2)}) collective-permute-start(bf16[128,1024]{1,0:T(8,128)(2,1)S(1)} %collective-permute-done.4), channel_id=1, source_target_pairs={{4,0},{8,4},{12,8},{16,12},{20,16},{24,20},{28,24},{0,28},{5,1},{9... | collective-permute-start | bytes 786440 | tf_op jit(solution)/shard_map/ppermute | solution.py:14
  52.8 2.2 %copy-start = (bf16[128,1024]{1,0:T(8,128)(2,1)S(1)}, bf16[128,1024]{1,0:T(8,128)(2,1)}, u32[]{:S(2)}) copy-start(bf16[128,1024]{1,0:T(8,128)(2,1)} %param.2) | copy-start | bytes 786436
where the time goes:
time: 71.7 us; the launch traced here: 71.4 us
  blocking collectives  40.5 us (56%)
  matrix products  11 us (15%)
  starting transfers between devices  8.13 us (11%)
  waiting for transfers between devices  7.96 us (11%)
  other arithmetic  3.69 us (5%)
    psum x1, blocking collectives, on_device(): pivots = lax.psum(local_rows, 'vec')  29.4 us
    all_gather x1, blocking collectives, on_device(): gram_all = lax.all_gather(gram_all, 'rep', axis=1, tiled=True)  11 us
    dot_general x14, matrix products, contract(): lax.dot_general(left, right, (((1,), (1,)), ((), ())), preferred_element_...  9.87 us
    ppermute x6, starting transfers between devices, from_behind(): return lax.ppermute(block, axis, route)  8.13 us
    ppermute x6, waiting for transfers between devices, from_behind(): return lax.ppermute(block, axis, route)  7.96 us
    convert_element_type x1, other arithmetic, on_device(): return similarity.astype(jnp.bfloat16)  1.9 us
  transfers between devices with their start and end apart: 6, of which 2 were waited for; matrix products, arithmetic and copies ran while one was open for 15% of the time, Pallas kernels for 0%

commit v1 on v0

v1 whole, which is shorter than its diff:
```python
import functools
import math

import jax
import jax.numpy as jnp
from jax import lax
from jax.experimental import pallas as pl
from jax.experimental.pallas import tpu as pltpu
from jax.sharding import PartitionSpec as P

HALF = 3
NEAR = 2


def contract(left, right):
    return lax.dot_general(
        left, right, (((1,), (1,)), ((), ())), preferred_element_type=jnp.float32
    )


def kernel(
    n_vec, n_a, n_b, vec_ref, index_ref, out_ref, win, rows_ref, heard, scaled,
    z_send, z_recv, d_send, d_recv, r_send, r_recv, p_send, p_recv, c_send, c_recv, own_sem,
):
    block_rows, fields = vec_ref.shape
    count = index_ref.shape[1]
    n_rep = n_a * n_b
    part = block_rows // n_rep
    half = fields // 2
    me = lax.axis_index("vec")
    rep = lax.axis_index("rep")
    a, b = rep // n_b, rep % n_b
    core = me % 2
    partner = me + 1 - 2 * core

    def at_vec(offset):
        return (me + offset + n_vec) % n_vec

    def rep_of(da, db):
        return ((a + da + n_a) % n_a) * n_b + (b + db + n_b) % n_b

    direct = [(0, i) for i in range(1, n_b)] + [(i, 0) for i in range(1, n_a)]
    diagonal = [(i, j) for i in range(1, n_a) for j in range(1, n_b)]

    barrier = pltpu.get_barrier_semaphore()

    def greet(i, carry):
        pl.semaphore_signal(barrier, inc=1, device_id={"vec": (me + i) % n_vec})
        return carry

    lax.fori_loop(1, n_vec, greet, 0, unroll=n_vec <= 16)
    for da, db in direct:
        pl.semaphore_signal(barrier, inc=1, device_id={"rep": rep_of(da, db)})

    own_copy = pltpu.make_async_copy(vec_ref, win.at[0], own_sem)
    own_copy.start()
    wanted = index_ref[...] - me * block_rows
    spots = lax.broadcasted_iota(jnp.int32, (block_rows, count), 0)
    onehot = (spots == wanted).astype(jnp.bfloat16)
    mine = lax.dot_general(
        onehot, vec_ref[...], (((0,), (0,)), ((), ())), preferred_element_type=jnp.float32
    )
    rows_ref[...] = mine.astype(jnp.bfloat16)
    pl.semaphore_wait(barrier, n_vec - 1 + len(direct))

    started = []

    def remote(src, dst, send_sem, recv_sem, device):
        copy = pltpu.make_async_remote_copy(
            src_ref=src, dst_ref=dst, send_sem=send_sem, recv_sem=recv_sem, device_id=device
        )
        copy.start()
        started.append(copy)
        return copy

    own_rows = pl.ds(pl.multiple_of(rep * part, part), part)
    far = 4 * (2 * core - 1)
    z_copies = []
    for s, offset in enumerate((2, -2, far)):
        z_copies.append(
            remote(
                vec_ref.at[own_rows], win.at[2 + s, own_rows], z_send.at[s], z_recv.at[s],
                {"vec": at_vec(offset)},
            )
        )
    partner_own = remote(vec_ref, win.at[1], c_send.at[0], c_recv.at[0], {"vec": partner})

    def pivot_copy(i):
        return pltpu.make_async_remote_copy(
            src_ref=rows_ref, dst_ref=heard.at[i], send_sem=p_send.at[i], recv_sem=p_recv.at[i],
            device_id={"vec": (me + i + 1) % n_vec},
        )

    def send_pivots(i, carry):
        pivot_copy(i).start()
        return carry

    def take_pivots(i, carry):
        pivot_copy(i).wait()
        return carry

    lax.fori_loop(0, n_vec - 1, send_pivots, 0, unroll=n_vec <= 16)

    per_slot = 1 + len(direct) + 2 * len(diagonal)
    across = [[] for _ in range(3)]

    def hand_over(s, rows, columns, number):
        k = 1 + s * per_slot + number
        across[s].append(
            remote(
                win.at[2 + s, rows, columns], win.at[5 + s, rows, columns],
                c_send.at[k], c_recv.at[k], {"vec": partner},
            )
        )

    everything = pl.ds(0, fields)
    first, second = pl.ds(0, half), pl.ds(half, half)

    def rows_from(da, db):
        return pl.ds(pl.multiple_of(rep_of(-da, -db) * part, part), part)

    d_copies = [[] for _ in range(3)]
    for s in range(3):
        z_copies[s].wait_recv()
        for t, (da, db) in enumerate(direct):
            d_copies[s].append(
                remote(
                    win.at[2 + s, own_rows], win.at[2 + s, own_rows],
                    d_send.at[s, t], d_recv.at[s, t], {"rep": rep_of(da, db)},
                )
            )
        hand_over(s, own_rows, everything, 0)

    r_copies = [[] for _ in range(3)]
    for s in range(3):
        for t, (da, db) in enumerate(direct):
            d_copies[s][t].wait_recv()
            rows = rows_from(da, db)
            if da == 0:
                onward = [((i, 0), first, 2 * diagonal.index((i, db))) for i in range(1, n_a)]
            else:
                onward = [((0, j), second, 2 * diagonal.index((da, j)) + 1) for j in range(1, n_b)]
            for (ra, rb), columns, number in onward:
                r_copies[s].append(
                    (
                        number,
                        remote(
                            win.at[2 + s, rows, columns], win.at[2 + s, rows, columns],
                            r_send.at[s, number], r_recv.at[s, number], {"rep": rep_of(ra, rb)},
                        ),
                    )
                )
            hand_over(s, rows, everything, 1 + t)

    lax.fori_loop(0, n_vec - 1, take_pivots, 0, unroll=n_vec <= 16)
    pivots = rows_ref[...].astype(jnp.float32)
    pivots = lax.fori_loop(
        0, n_vec - 1, lambda i, total: total + heard[i].astype(jnp.float32), pivots, unroll=n_vec <= 16
    )
    level = jnp.sum(pivots, axis=1, keepdims=True) / fields
    pivots = pivots - level
    own = vec_ref[...].astype(jnp.float32)
    for k in range(count):
        scaled[k * block_rows:(k + 1) * block_rows, :] = (own * pivots[k:k + 1, :]).astype(jnp.bfloat16)

    root = 1.0 / math.sqrt(fields)

    def compare(slot, width, offsets):
        right = win[slot:slot + width].reshape(width * block_rows, fields)
        value = (contract(scaled[...], right) * root).astype(jnp.bfloat16)
        for i, offset in enumerate(offsets):
            out_ref[HALF + offset] = value[:, i * block_rows:(i + 1) * block_rows].reshape(
                count, block_rows, block_rows
            )

    own_copy.wait()
    partner_own.wait_recv()
    compare(0, 2, (0, 1 - 2 * core))

    for s in range(3):
        for number, copy in sorted(r_copies[s], key=lambda pair: pair[0]):
            copy.wait_recv()
            da, db = diagonal[number // 2]
            hand_over(s, rows_from(da, db), (first, second)[number % 2], 1 + len(direct) + number)

    compare(2, 2, (-2, 2))
    for s in (0, 1):
        for copy in across[s]:
            copy.wait_recv()
    compare(5, 2, (-1 - 2 * core, 3 - 2 * core))
    for copy in across[2]:
        copy.wait_recv()
    compare(7, 1, (6 * core - 3,))
    for copy in started:
        copy.wait_send()


def solution(mesh):
    n_vec, n_rep = mesh.shape["vec"], mesh.shape["rep"]
    n_b = 2 if n_rep % 2 == 0 else 1
    n_a = n_rep // n_b
    assert n_vec % 2 == 0 and n_vec > 2 * HALF

    def step(vectors, pivot_index):
        rows, fields = vectors.shape
        count = pivot_index.shape[1]
        direct = n_a + n_b - 2
        diagonal = (n_a - 1) * (n_b - 1)
        dma = pltpu.SemaphoreType.DMA
        across = 1 + 3 * (1 + direct + 2 * diagonal)
        vmem = pl.BlockSpec(memory_space=pltpu.VMEM)
        return pl.pallas_call(
            functools.partial(kernel, n_vec, n_a, n_b),
            out_shape=jax.ShapeDtypeStruct((2 * HALF + 1, count, rows, rows), jnp.bfloat16),
            in_specs=[vmem, vmem],
            out_specs=vmem,
            scratch_shapes=[
                pltpu.VMEM((8, rows, fields), jnp.bfloat16),
                pltpu.VMEM((count, fields), jnp.bfloat16),
                pltpu.VMEM((n_vec - 1, count, fields), jnp.bfloat16),
                pltpu.VMEM((count * rows, fields), jnp.bfloat16),
                dma((3,)), dma((3,)),
                dma((3, max(direct, 1))), dma((3, max(direct, 1))),
                dma((3, max(2 * diagonal, 1))), dma((3, max(2 * diagonal, 1))),
                dma((n_vec - 1,)), dma((n_vec - 1,)),
                dma((across,)), dma((across,)),
                dma(()),
            ],
            compiler_params=pltpu.CompilerParams(collective_id=0, has_side_effects=True),
        )(vectors, pivot_index)

    return jax.shard_map(
        step, mesh=mesh, in_specs=(P("vec", None), P("rep", None)),
        out_specs=P(None, "rep", "vec", None), check_vma=False,
    )
```

time: 71.7 us -> 31.2 us (0.44)
  blocking collectives: 40.5 us -> 0 us
  Pallas kernels: 0 us -> 28.1 us
  matrix products: 11 us -> 0 us
  starting transfers between devices: 8.13 us -> 0 us
  waiting for transfers between devices: 7.96 us -> 0 us
  other arithmetic: 3.69 us -> 0 us
  local copies, waits for them, and re-layouts: 0.01 us -> 2.94 us
    psum x1 -> x0, blocking collectives: 29.4 us -> none  [on_device(): pivots = lax.psum(local_rows, 'vec')]
    pallas_call x0 -> x1, Pallas kernels: none -> 28.1 us  [step(): pl.pallas_call(functools.partial(kernel, n_vec, n_a, n_b), out_shape=jax....]
    all_gather x1 -> x0, blocking collectives: 11 us -> none  [on_device(): gram_all = lax.all_gather(gram_all, 'rep', axis=1, tiled=True)]
    dot_general x15 -> x0, matrix products: 11 us -> none  [the longest x14 9.87 us: contract(): lax.dot_general(left, right, (((1,), (1,)), ((), ())), preferred_element_...]
    ppermute x6 -> x0, starting transfers between devices: 8.13 us -> none  [from_behind(): return lax.ppermute(block, axis, route)]
    ppermute x6 -> x0, waiting for transfers between devices: 7.96 us -> none  [from_behind(): return lax.ppermute(block, axis, route)]
    unnamed x2 -> x1, local copies, waits for them, and re-layouts: 0.01 us -> 2.94 us
    convert_element_type x2 -> x0, other arithmetic: 2.9 us -> none  [the longest x1 1.9 us: on_device(): return similarity.astype(jnp.bfloat16)]
  transfers between devices with their start and end apart: 6 -> 0, of which waited for: 2 -> 0; matrix products, arithmetic and copies ran while one was open for 15% -> 0% of each run, Pallas kernels for 0% -> 0%
where the time goes in v1:
time: 31.2 us; the launch traced here: 31.1 us
  Pallas kernels  28.1 us (90%)
  local copies, waits for them, and re-layouts  2.94 us (9%)
    pallas_call x1, Pallas kernels, step(): pl.pallas_call(functools.partial(kernel, n_vec, n_a, n_b), out_shape=jax....  28.1 us
    unnamed x1, local copies, waits for them, and re-layouts  2.94 us

profile of v1, /device:TPU:0, one launch (start us, length us, event | category | flops | bytes accessed | tf_op | source)
XLA Modules:
  0.0 31.1 jit_solution(6876878989045942872)
XLA Ops:
  0.0 28.1 %shard_map.28 = bf16[7,8,128,128]{3,2,1,0:T(8,128)(2,1)} custom-call(bf16[128,1024]{1,0:T(8,128)(2,1)} %vec_ref.1, s32[1,8]{1,0:T(1,128)} %index_ref.1), custom_call_target="tpu_custom_call" | custom-call | tf_op jit(solution)/shard_map/pallas_call | solution.py:212
  28.1 2.9 %copy.4 = bf16[7,8,128,128]{3,2,1,0:T(8,128)(2,1)} copy(bf16[7,8,128,128]{3,2,1,0:T(8,128)(2,1)} %shard_map.28) | data formatting | bytes 3670016

commit v2 on v0

v2 whole, which is shorter than its diff:
```python
import functools
import math

import jax
import jax.numpy as jnp
from jax import lax
from jax.experimental import pallas as pl
from jax.experimental.pallas import tpu as pltpu
from jax.sharding import PartitionSpec as P

HALF = 3


def contract(left, right):
    return lax.dot_general(
        left, right, (((1,), (1,)), ((), ())), preferred_element_type=jnp.float32
    )


def kernel(
    n_vec, n_a, n_b, vec_ref, index_ref, out_ref, win, wanted_ref, rows_ref, heard, scaled,
    z_send, z_recv, d_send, d_recv, r_send, r_recv, p_send, p_recv, c_send, c_recv, local_sem,
):
    block_rows, fields = vec_ref.shape
    count = index_ref.shape[1]
    n_rep = n_a * n_b
    chips = n_vec // 2
    part = block_rows // n_rep
    half = fields // 2
    me = lax.axis_index("vec")
    rep = lax.axis_index("rep")
    a, b = rep // n_b, rep % n_b
    chip, core = me // 2, me % 2
    partner = me + 1 - 2 * core

    def at_vec(offset):
        return {"vec": (me + offset + n_vec) % n_vec}

    def rep_of(da, db):
        return ((a + da + n_a) % n_a) * n_b + (b + db + n_b) % n_b

    direct = [(0, i) for i in range(1, n_b)] + [(i, 0) for i in range(1, n_a)]
    diagonal = [(i, j) for i in range(1, n_a) for j in range(1, n_b)]
    short = n_vec <= 16

    own_copy = pltpu.make_async_copy(vec_ref, win.at[0], local_sem.at[0])
    index_copy = pltpu.make_async_copy(index_ref, wanted_ref, local_sem.at[1])
    own_copy.start()
    index_copy.start()

    barrier = pltpu.get_barrier_semaphore()

    def greet(i, carry):
        pl.semaphore_signal(barrier, inc=1, device_id=at_vec(2 * i))
        return carry

    lax.fori_loop(1, chips, greet, 0, unroll=short)
    pl.semaphore_signal(barrier, inc=1, device_id={"vec": partner})
    for da, db in direct:
        pl.semaphore_signal(barrier, inc=1, device_id={"rep": rep_of(da, db)})
    own_copy.wait()
    index_copy.wait()
    pl.semaphore_wait(barrier, chips + len(direct))

    def remote(src, dst, send_sem, recv_sem, device):
        return pltpu.make_async_remote_copy(
            src_ref=src, dst_ref=dst, send_sem=send_sem, recv_sem=recv_sem, device_id=device
        )

    started = []

    def start(copy):
        copy.start()
        started.append(copy)

    own_rows = pl.ds(pl.multiple_of(rep * part, part), part)
    far = 4 * (2 * core - 1)
    first_chip = 1 - (chip + chips - 1) // chips
    last_chip = (chip + 1) // chips
    edge = first_chip + last_chip
    outgoing = (last_chip, 1 + edge, 2 - 2 * edge + first_chip)
    order = (first_chip, 1 + edge, 2 - 2 * edge + last_chip)

    def z_copy(s):
        is_far = s // 2
        offset = (2 - 4 * s) * (1 - is_far) + far * is_far
        return remote(
            win.at[0, own_rows], win.at[2 + 2 * s, own_rows], z_send.at[s], z_recv.at[s], at_vec(offset)
        )

    for s in outgoing:
        start(z_copy(s))
    partner_own = remote(win.at[0], win.at[1], c_send.at[0], c_recv.at[0], {"vec": partner})
    start(partner_own)

    wanted = wanted_ref[...] - me * block_rows
    spots = lax.broadcasted_iota(jnp.int32, (block_rows, count), 0)
    onehot = (spots == wanted).astype(jnp.bfloat16)
    mine = lax.dot_general(
        onehot, win[0], (((0,), (0,)), ((), ())), preferred_element_type=jnp.float32
    )
    rows_ref[...] = mine.astype(jnp.bfloat16)

    def rows_out(i):
        return remote(rows_ref, heard.at[i], p_send.at[i], p_recv.at[i], at_vec(2 * i))

    rows_partner = remote(rows_ref, heard.at[0], p_send.at[0], p_recv.at[0], {"vec": partner})

    def rows_across(i):
        k = chips - 1 + i
        return remote(heard.at[i], heard.at[k], p_send.at[k], p_recv.at[k], {"vec": partner})

    def loop(action):
        def body(i, carry):
            action(i)
            return carry

        lax.fori_loop(1, chips, body, 0, unroll=short)

    per_slot = 1 + len(direct) + 2 * len(diagonal)
    everything = pl.ds(0, fields)
    halves = (pl.ds(0, half), pl.ds(half, half))

    def rows_from(da, db):
        return pl.ds(pl.multiple_of(rep_of(-da, -db) * part, part), part)

    def hand(s, number):
        if number == 0:
            rows, columns = own_rows, everything
        elif number <= len(direct):
            rows, columns = rows_from(*direct[number - 1]), everything
        else:
            which = number - 1 - len(direct)
            rows, columns = rows_from(*diagonal[which // 2]), halves[which % 2]
        k = 1 + s * per_slot + number
        return remote(
            win.at[2 + 2 * s, rows, columns], win.at[3 + 2 * s, rows, columns],
            c_send.at[k], c_recv.at[k], {"vec": partner},
        )

    def d_copy(s, t):
        slot = win.at[2 + 2 * s, own_rows]
        return remote(slot, slot, d_send.at[s, t], d_recv.at[s, t], {"rep": rep_of(*direct[t])})

    def r_copy(s, t, hop, number):
        slot = win.at[2 + 2 * s, rows_from(*direct[t]), halves[number % 2]]
        return remote(slot, slot, r_send.at[s, number], r_recv.at[s, number], {"rep": rep_of(*hop)})

    def relays(t):
        da, db = direct[t]
        if da == 0:
            return [((i, 0), 2 * diagonal.index((i, db))) for i in range(1, n_a)]
        return [((0, j), 2 * diagonal.index((da, j)) + 1) for j in range(1, n_b)]

    def after_z(s):
        z_copy(s).wait_recv()
        for t in range(len(direct)):
            start(d_copy(s, t))
        start(hand(s, 0))

    def after_direct(s):
        for t in range(len(direct)):
            d_copy(s, t).wait_recv()
            for hop, number in relays(t):
                start(r_copy(s, t, hop, number))
            start(hand(s, 1 + t))

    def after_relay(s):
        for number in range(2 * len(diagonal)):
            slot = win.at[2 + 2 * s, rows_from(*diagonal[number // 2]), halves[number % 2]]
            remote(
                slot, slot, r_send.at[s, number], r_recv.at[s, number], {"vec": partner}
            ).wait_recv()
            start(hand(s, 1 + len(direct) + number))

    root = 1.0 / math.sqrt(fields)

    def compare(slot):
        right = win[pl.ds(slot, 2)].reshape(2 * block_rows, fields)
        value = (contract(scaled[...], right) * root).astype(jnp.bfloat16)
        shape = (count, block_rows, block_rows)
        return value[:, :block_rows].reshape(shape), value[:, block_rows:].reshape(shape)

    def finish(s):
        for number in range(per_slot):
            hand(s, number).wait_recv()
        is_far = s // 2
        left, right = compare(2 + 2 * s)

        @pl.when(is_far == 0)
        def _():
            out_ref[HALF + (4 * s - 2) * (1 - is_far)] = left

        out_ref[HALF + (4 * s - 1 - 2 * core) * (1 - is_far) + (6 * core - 3) * is_far] = right

    after_z(order[0])
    start(rows_partner)
    loop(lambda i: rows_out(i).start())
    after_z(order[1])
    after_direct(order[0])
    after_z(order[2])
    after_direct(order[1])

    def pass_rows(i):
        rows_out(i).wait_recv()
        rows_across(i).start()

    loop(pass_rows)
    after_direct(order[2])
    after_relay(order[0])

    rows_partner.wait_recv()
    loop(lambda i: rows_across(i).wait_recv())
    pivots = lax.fori_loop(
        0, n_vec - 1, lambda i, total: total + heard[i].astype(jnp.float32),
        rows_ref[...].astype(jnp.float32), unroll=short,
    )
    level = jnp.sum(pivots, axis=1, keepdims=True) / fields
    pivots = pivots - level
    own = win[0].astype(jnp.float32)
    for k in range(count):
        scaled[k * block_rows:(k + 1) * block_rows, :] = (own * pivots[k:k + 1, :]).astype(jnp.bfloat16)

    partner_own.wait_recv()
    left, right = compare(0)
    out_ref[HALF] = left
    out_ref[HALF + 1 - 2 * core] = right
    after_relay(order[1])
    finish(order[0])
    after_relay(order[2])
    finish(order[1])
    finish(order[2])
    for copy in started:
        copy.wait_send()
    loop(lambda i: rows_out(i).wait_send())
    loop(lambda i: rows_across(i).wait_send())


def solution(mesh):
    n_vec, n_rep = mesh.shape["vec"], mesh.shape["rep"]
    n_b = 2 if n_rep % 2 == 0 else 1
    n_a = n_rep // n_b
    assert n_vec % 2 == 0 and n_vec > 2 * HALF

    def step(vectors, pivot_index):
        rows, fields = vectors.shape
        count = pivot_index.shape[1]
        direct = n_a + n_b - 2
        diagonal = (n_a - 1) * (n_b - 1)
        dma = pltpu.SemaphoreType.DMA
        across = 1 + 3 * (1 + direct + 2 * diagonal)
        vmem = pl.BlockSpec(memory_space=pltpu.VMEM)
        hbm = pl.BlockSpec(memory_space=pltpu.HBM)
        return pl.pallas_call(
            functools.partial(kernel, n_vec, n_a, n_b),
            out_shape=jax.ShapeDtypeStruct((2 * HALF + 1, count, rows, rows), jnp.bfloat16),
            in_specs=[hbm, hbm],
            out_specs=vmem,
            scratch_shapes=[
                pltpu.VMEM((8, rows, fields), jnp.bfloat16),
                pltpu.VMEM((1, count), jnp.int32),
                pltpu.VMEM((count, fields), jnp.bfloat16),
                pltpu.VMEM((n_vec - 1, count, fields), jnp.bfloat16),
                pltpu.VMEM((count * rows, fields), jnp.bfloat16),
                dma((3,)), dma((3,)),
                dma((3, max(direct, 1))), dma((3, max(direct, 1))),
                dma((3, max(2 * diagonal, 1))), dma((3, max(2 * diagonal, 1))),
                dma((n_vec - 1,)), dma((n_vec - 1,)),
                dma((across,)), dma((across,)),
                dma((2,)),
            ],
            compiler_params=pltpu.CompilerParams(
                collective_id=0, has_side_effects=True, vmem_limit_bytes=24 * 2**20
            ),
        )(vectors, pivot_index)

    return jax.shard_map(
        step, mesh=mesh, in_specs=(P("vec", None), P("rep", None)),
        out_specs=P(None, "rep", "vec", None), check_vma=False,
    )
```

time: 71.7 us -> 27.6 us (0.38)
  blocking collectives: 40.5 us -> 0 us
  Pallas kernels: 0 us -> 24.6 us
  matrix products: 11 us -> 0 us
  starting transfers between devices: 8.13 us -> 0 us
  waiting for transfers between devices: 7.96 us -> 0 us
  other arithmetic: 3.69 us -> 0 us
  local copies, waits for them, and re-layouts: 0.01 us -> 2.84 us
    psum x1 -> x0, blocking collectives: 29.4 us -> none  [on_device(): pivots = lax.psum(local_rows, 'vec')]
    pallas_call x0 -> x1, Pallas kernels: none -> 24.6 us  [step(): pl.pallas_call(functools.partial(kernel, n_vec, n_a, n_b), out_shape=jax....]
    all_gather x1 -> x0, blocking collectives: 11 us -> none  [on_device(): gram_all = lax.all_gather(gram_all, 'rep', axis=1, tiled=True)]
    dot_general x15 -> x0, matrix products: 11 us -> none  [the longest x14 9.87 us: contract(): lax.dot_general(left, right, (((1,), (1,)), ((), ())), preferred_element_...]
    ppermute x6 -> x0, starting transfers between devices: 8.13 us -> none  [from_behind(): return lax.ppermute(block, axis, route)]
    ppermute x6 -> x0, waiting for transfers between devices: 7.96 us -> none  [from_behind(): return lax.ppermute(block, axis, route)]
    convert_element_type x2 -> x0, other arithmetic: 2.9 us -> none  [the longest x1 1.9 us: on_device(): return similarity.astype(jnp.bfloat16)]
    unnamed x2 -> x5, local copies, waits for them, and re-layouts: 0.01 us -> 2.84 us
  transfers between devices with their start and end apart: 6 -> 0, of which waited for: 2 -> 0; matrix products, arithmetic and copies ran while one was open for 15% -> 0% of each run, Pallas kernels for 0% -> 0%
where the time goes in v2:
time: 27.6 us; the launch traced here: 27.5 us
  Pallas kernels  24.6 us (89%)
  local copies, waits for them, and re-layouts  2.84 us (10%)
    pallas_call x1, Pallas kernels, step(): pl.pallas_call(functools.partial(kernel, n_vec, n_a, n_b), out_shape=jax....  24.6 us
    unnamed x5, local copies, waits for them, and re-layouts  2.84 us

profile of v2, /device:TPU:0, one launch (start us, length us, event | category | flops | bytes accessed | tf_op | source)
XLA Modules:
  0.0 27.5 jit_solution(6091343270227708522)
XLA Ops:
  0.0 0.0 copy-start
  0.0 0.9 %copy-done = bf16[128,1024]{1,0:T(8,128)(2,1)S(1)} copy-done((bf16[128,1024]{1,0:T(8,128)(2,1)S(1)}, bf16[128,1024]{1,0:T(8,128)(2,1)}, u32[]{:S(2)}) %copy-start) | copy-done | bytes 262168
  1.0 0.0 copy-start.1
  1.0 0.7 %copy-done.1 = s32[1,8]{1,0:T(1,128)S(1)} copy-done((s32[1,8]{1,0:T(1,128)S(1)}, s32[1,8]{1,0:T(1,128)}, u32[]{:S(2)}) %copy-start.1) | copy-done | bytes 56
  1.6 24.6 %shard_map.28 = bf16[7,8,128,128]{3,2,1,0:T(8,128)(2,1)S(1)} custom-call(bf16[128,1024]{1,0:T(8,128)(2,1)S(1)} %copy-done, s32[1,8]{1,0:T(1,128)S(1)} %copy-done.1), custom_call_target="tpu_custom_call" | custom-call | tf_op jit(solution)/shard_map/pallas_call | solution.py:254
  26.3 1.2 %copy.4 = bf16[7,8,128,128]{3,2,1,0:T(8,128)(2,1)} copy(bf16[7,8,128,128]{3,2,1,0:T(8,128)(2,1)S(1)} %shard_map.28) | data formatting | bytes 3670016
Async XLA Ops:
  0.0 0.9 %copy-start = (bf16[128,1024]{1,0:T(8,128)(2,1)S(1)}, bf16[128,1024]{1,0:T(8,128)(2,1)}, u32[]{:S(2)}) copy-start(bf16[128,1024]{1,0:T(8,128)(2,1)} %vec_ref.1) | copy-start | bytes 786436
  1.0 0.7 %copy-start.1 = (s32[1,8]{1,0:T(1,128)S(1)}, s32[1,8]{1,0:T(1,128)}, u32[]{:S(2)}) copy-start(s32[1,8]{1,0:T(1,128)} %index_ref.1) | copy-start | bytes 100

commit v3 on v2

--- a/solution.py
+++ b/solution.py
@@ -26,7 +26,6 @@
     n_rep = n_a * n_b
     chips = n_vec // 2
     part = block_rows // n_rep
-    half = fields // 2
     me = lax.axis_index("vec")
     rep = lax.axis_index("rep")
     a, b = rep // n_b, rep % n_b
@@ -119,10 +118,13 @@
 
     per_slot = 1 + len(direct) + 2 * len(diagonal)
     everything = pl.ds(0, fields)
-    halves = (pl.ds(0, half), pl.ds(half, half))
 
     def rows_from(da, db):
         return pl.ds(pl.multiple_of(rep_of(-da, -db) * part, part), part)
+
+    def half_from(da, db, h):
+        start_row = rep_of(-da, -db) * part + h * (part // 2)
+        return pl.ds(pl.multiple_of(start_row, part // 2), part // 2)
 
     def hand(s, number):
         if number == 0:
@@ -131,19 +133,25 @@
             rows, columns = rows_from(*direct[number - 1]), everything
         else:
             which = number - 1 - len(direct)
-            rows, columns = rows_from(*diagonal[which // 2]), halves[which % 2]
+            rows, columns = half_from(*diagonal[which // 2], which % 2), everything
         k = 1 + s * per_slot + number
         return remote(
             win.at[2 + 2 * s, rows, columns], win.at[3 + 2 * s, rows, columns],
             c_send.at[k], c_recv.at[k], {"vec": partner},
         )
 
+    def hand_all(s):
+        k = 1 + s * per_slot
+        return remote(
+            win.at[2 + 2 * s], win.at[3 + 2 * s], c_send.at[k], c_recv.at[k], {"vec": partner}
+        )
+
     def d_copy(s, t):
         slot = win.at[2 + 2 * s, own_rows]
         return remote(slot, slot, d_send.at[s, t], d_recv.at[s, t], {"rep": rep_of(*direct[t])})
 
     def r_copy(s, t, hop, number):
-        slot = win.at[2 + 2 * s, rows_from(*direct[t]), halves[number % 2]]
+        slot = win.at[2 + 2 * s, half_from(*direct[t], number % 2)]
         return remote(slot, slot, r_send.at[s, number], r_recv.at[s, number], {"rep": rep_of(*hop)})
 
     def relays(t):
@@ -156,22 +164,20 @@
         z_copy(s).wait_recv()
         for t in range(len(direct)):
             start(d_copy(s, t))
-        start(hand(s, 0))
 
     def after_direct(s):
         for t in range(len(direct)):
             d_copy(s, t).wait_recv()
             for hop, number in relays(t):
                 start(r_copy(s, t, hop, number))
-            start(hand(s, 1 + t))
 
     def after_relay(s):
         for number in range(2 * len(diagonal)):
-            slot = win.at[2 + 2 * s, rows_from(*diagonal[number // 2]), halves[number % 2]]
+            slot = win.at[2 + 2 * s, half_from(*diagonal[number // 2], number % 2)]
             remote(
                 slot, slot, r_send.at[s, number], r_recv.at[s, number], {"vec": partner}
             ).wait_recv()
-            start(hand(s, 1 + len(direct) + number))
+        start(hand_all(s))
 
     root = 1.0 / math.sqrt(fields)
 
@@ -182,8 +188,7 @@
         return value[:, :block_rows].reshape(shape), value[:, block_rows:].reshape(shape)
 
     def finish(s):
-        for number in range(per_slot):
-            hand(s, number).wait_recv()
+        hand_all(s).wait_recv()
         is_far = s // 2
         left, right = compare(2 + 2 * s)
 
@@ -253,7 +258,7 @@
         hbm = pl.BlockSpec(memory_space=pltpu.HBM)
         return pl.pallas_call(
             functools.partial(kernel, n_vec, n_a, n_b),
-            out_shape=jax.ShapeDtypeStruct((2 * HALF + 1, count, rows, rows), jnp.bfloat16),
+            out_shape=pltpu.VMEM((2 * HALF + 1, count, rows, rows), jnp.bfloat16),
             in_specs=[hbm, hbm],
             out_specs=vmem,
             scratch_shapes=[
@@ -270,7 +275,7 @@
                 dma((2,)),
             ],
             compiler_params=pltpu.CompilerParams(
-                collective_id=0, has_side_effects=True, vmem_limit_bytes=24 * 2**20
+                collective_id=0, has_side_effects=True, vmem_limit_bytes=65_000_000
             ),
         )(vectors, pivot_index)
 

time: 27.6 us -> 25.9 us (0.938)
  local copies, waits for them, and re-layouts: 2.84 us -> 1.23 us
    unnamed x5 -> x1, local copies, waits for them, and re-layouts: 2.84 us -> 1.23 us
where the time goes in v3:
time: 25.9 us; the launch traced here: 25.8 us
  Pallas kernels  24.5 us (95%)
  local copies, waits for them, and re-layouts  1.23 us (5%)
    pallas_call x1, Pallas kernels, step(): pl.pallas_call(functools.partial(kernel, n_vec, n_a, n_b), out_shape=pltp...  24.5 us
    unnamed x1, local copies, waits for them, and re-layouts  1.23 us

profile of v3, /device:TPU:0, one launch (start us, length us, event | category | flops | bytes accessed | tf_op | source)
XLA Modules:
  0.0 25.8 jit_solution(3118626893578199328)
XLA Ops:
  0.0 24.5 %shard_map.28 = bf16[7,8,128,128]{3,2,1,0:T(8,128)(2,1)S(1)} custom-call(bf16[128,1024]{1,0:T(8,128)(2,1)} %vec_ref.1, s32[1,8]{1,0:T(1,128)} %index_ref.1), custom_call_target="tpu_custom_call" | custom-call | tf_op jit(solution)/shard_map/pallas_call | solution.py:259
  24.5 1.2 %copy.4 = bf16[7,8,128,128]{3,2,1,0:T(8,128)(2,1)} copy(bf16[7,8,128,128]{3,2,1,0:T(8,128)(2,1)S(1)} %shard_map.28) | data formatting | bytes 3670016

commit v4 on v3

--- a/solution.py
+++ b/solution.py
@@ -17,8 +17,57 @@
     )
 
 
+def arrival(chip, chips):
+    first_chip = 1 - (chip + chips - 1) // chips
+    last_chip = (chip + 1) // chips
+    edge = first_chip + last_chip
+    return first_chip, last_chip, edge, (first_chip, 1 + edge, 2 - 2 * edge + last_chip)
+
+
+def places(s, core):
+    is_far = s // 2
+    own = HALF + (4 * s - 2) * (1 - is_far)
+    other = HALF + (4 * s - 1 - 2 * core) * (1 - is_far) + (6 * core - 3) * is_far
+    return is_far, own, other
+
+
+def products(scaled, win, slot, count, block_rows):
+    fields = scaled.shape[1]
+    right = win[pl.ds(slot, 2)].reshape(2 * block_rows, fields)
+    value = (contract(scaled[...], right) * (1.0 / math.sqrt(fields))).astype(jnp.bfloat16)
+    shape = (count, block_rows, block_rows)
+    return value[:, :block_rows].reshape(shape), value[:, block_rows:].reshape(shape)
+
+
+def closing(n_vec, held, win, scaled, out_ref, last, sems):
+    window, count, block_rows, _ = held.shape
+    me = lax.axis_index("vec")
+    core = me % 2
+    s = arrival(me // 2, n_vec // 2)[3][2]
+    is_far, own, other = places(s, core)
+    own = own * (1 - is_far) + other * is_far
+
+    def ready(i):
+        return pltpu.make_async_copy(held.at[i], out_ref.at[i], sems.at[i])
+
+    def late(i, place):
+        return pltpu.make_async_copy(last.at[i], out_ref.at[place], sems.at[window + i])
+
+    for i in range(window):
+        pl.when(jnp.logical_and(own != i, other != i))(lambda i=i: ready(i).start())
+    left, right = products(scaled, win, 2 + 2 * s, count, block_rows)
+    last[0] = left
+    last[1] = right
+    pl.when(is_far == 0)(lambda: late(0, own).start())
+    late(1, other).start()
+    for i in range(window):
+        pl.when(jnp.logical_and(own != i, other != i))(lambda i=i: ready(i).wait())
+    pl.when(is_far == 0)(lambda: late(0, own).wait())
+    late(1, other).wait()
+
+
 def kernel(
-    n_vec, n_a, n_b, vec_ref, index_ref, out_ref, win, wanted_ref, rows_ref, heard, scaled,
+    n_vec, n_a, n_b, vec_ref, index_ref, out_ref, win, scaled, wanted_ref, rows_ref, heard,
     z_send, z_recv, d_send, d_recv, r_send, r_recv, p_send, p_recv, c_send, c_recv, local_sem,
 ):
     block_rows, fields = vec_ref.shape
@@ -74,11 +123,8 @@
 
     own_rows = pl.ds(pl.multiple_of(rep * part, part), part)
     far = 4 * (2 * core - 1)
-    first_chip = 1 - (chip + chips - 1) // chips
-    last_chip = (chip + 1) // chips
-    edge = first_chip + last_chip
+    first_chip, last_chip, edge, order = arrival(chip, chips)
     outgoing = (last_chip, 1 + edge, 2 - 2 * edge + first_chip)
-    order = (first_chip, 1 + edge, 2 - 2 * edge + last_chip)
 
     def z_copy(s):
         is_far = s // 2
@@ -179,24 +225,19 @@
             ).wait_recv()
         start(hand_all(s))
 
-    root = 1.0 / math.sqrt(fields)
-
     def compare(slot):
-        right = win[pl.ds(slot, 2)].reshape(2 * block_rows, fields)
-        value = (contract(scaled[...], right) * root).astype(jnp.bfloat16)
-        shape = (count, block_rows, block_rows)
-        return value[:, :block_rows].reshape(shape), value[:, block_rows:].reshape(shape)
+        return products(scaled, win, slot, count, block_rows)
 
     def finish(s):
         hand_all(s).wait_recv()
-        is_far = s // 2
+        is_far, below, above = places(s, core)
         left, right = compare(2 + 2 * s)
 
         @pl.when(is_far == 0)
         def _():
-            out_ref[HALF + (4 * s - 2) * (1 - is_far)] = left
-
-        out_ref[HALF + (4 * s - 1 - 2 * core) * (1 - is_far) + (6 * core - 3) * is_far] = right
+            out_ref[below] = left
+
+        out_ref[above] = right
 
     after_z(order[0])
     start(rows_partner)
@@ -234,7 +275,7 @@
     finish(order[0])
     after_relay(order[2])
     finish(order[1])
-    finish(order[2])
+    hand_all(order[2]).wait_recv()
     for copy in started:
         copy.wait_send()
     loop(lambda i: rows_out(i).wait_send())
@@ -256,17 +297,19 @@
         across = 1 + 3 * (1 + direct + 2 * diagonal)
         vmem = pl.BlockSpec(memory_space=pltpu.VMEM)
         hbm = pl.BlockSpec(memory_space=pltpu.HBM)
-        return pl.pallas_call(
+        held, win, scaled = pl.pallas_call(
             functools.partial(kernel, n_vec, n_a, n_b),
-            out_shape=pltpu.VMEM((2 * HALF + 1, count, rows, rows), jnp.bfloat16),
+            out_shape=(
+                pltpu.VMEM((2 * HALF + 1, count, rows, rows), jnp.bfloat16),
+                pltpu.VMEM((8, rows, fields), jnp.bfloat16),
+                pltpu.VMEM((count * rows, fields), jnp.bfloat16),
+            ),
             in_specs=[hbm, hbm],
-            out_specs=vmem,
+            out_specs=(vmem, vmem, vmem),
             scratch_shapes=[
-                pltpu.VMEM((8, rows, fields), jnp.bfloat16),
                 pltpu.VMEM((1, count), jnp.int32),
                 pltpu.VMEM((count, fields), jnp.bfloat16),
                 pltpu.VMEM((n_vec - 1, count, fields), jnp.bfloat16),
-                pltpu.VMEM((count * rows, fields), jnp.bfloat16),
                 dma((3,)), dma((3,)),
                 dma((3, max(direct, 1))), dma((3, max(direct, 1))),
                 dma((3, max(2 * diagonal, 1))), dma((3, max(2 * diagonal, 1))),
@@ -275,9 +318,19 @@
                 dma((2,)),
             ],
             compiler_params=pltpu.CompilerParams(
-                collective_id=0, has_side_effects=True, vmem_limit_bytes=65_000_000
+                collective_id=0, has_side_effects=True, vmem_limit_bytes=60_800_000
             ),
         )(vectors, pivot_index)
+        return pl.pallas_call(
+            functools.partial(closing, n_vec),
+            out_shape=jax.ShapeDtypeStruct(held.shape, held.dtype),
+            in_specs=[vmem, vmem, vmem],
+            out_specs=pl.BlockSpec(memory_space=pl.ANY),
+            scratch_shapes=[
+                pltpu.VMEM((2, *held.shape[1:]), held.dtype), dma((2 * HALF + 3,)),
+            ],
+            compiler_params=pltpu.CompilerParams(vmem_limit_bytes=24 * 2**20),
+        )(held, win, scaled)
 
     return jax.shard_map(
         step, mesh=mesh, in_specs=(P("vec", None), P("rep", None)),

time: 25.9 us -> 25.3 us (0.977)
  local copies, waits for them, and re-layouts: 1.23 us -> 0 us
  Pallas kernels: 24.5 us -> 25.2 us
    unnamed x1 -> x0, local copies, waits for them, and re-layouts: 1.23 us -> none
    pallas_call x1 -> x2, Pallas kernels: 24.5 us -> 25.2 us  [the longest x1 23.2 us: step(): pl.pallas_call(functools.partial(kernel, n_vec, n_a, n_b), out_shape=(plt...]
where the time goes in v4:
time: 25.3 us; the launch traced here: 25.2 us
  Pallas kernels  25.2 us (100%)
    pallas_call x1, Pallas kernels, step(): pl.pallas_call(functools.partial(kernel, n_vec, n_a, n_b), out_shape=(plt...  23.2 us
    pallas_call x1, Pallas kernels, step(): pl.pallas_call(functools.partial(closing, n_vec), out_shape=jax.ShapeDtyp...  1.95 us

profile of v4, /device:TPU:0, one launch (start us, length us, event | category | flops | bytes accessed | tf_op | source)
XLA Modules:
  0.0 25.2 jit_solution(12531760314797311370)
XLA Ops:
  0.0 23.2 %shard_map.28 = (bf16[7,8,128,128]{3,2,1,0:T(8,128)(2,1)S(1)}, bf16[8,128,1024]{2,1,0:T(8,128)(2,1)S(1)}, bf16[1024,1024]{1,0:T(8,128)(2,1)S(1)}) custom-call(bf16[128,1024]{1,0:T(8,128)(2,1)} %vec_ref.1, s32[1,8]{1,0:T(1,128)} %index_ref.1), custom_call_target="tpu_custom_call" | custom-call | tf_op jit(solution)/shard_map/pallas_call | solution.py:300
  23.2 1.9 %shard_map.29 = bf16[7,8,128,128]{3,2,1,0:T(8,128)(2,1)} custom-call(bf16[7,8,128,128]{3,2,1,0:T(8,128)(2,1)S(1)} %get-tuple-element.8.held, bf16[8,128,1024]{2,1,0:T(8,128)(2,1)S(1)} %get-tuple-element.9.win, bf16[1024,1024]{1,0:T(8,128)(2,1)S(1)} %get-tuple-element.10.scaled), custom_call_target="tpu_custom_call" | custom-call | tf_op jit(solution)/shard_map/pallas_call | solution.py:324
